TPU v7x, 32 devices: a whole 2x2x4 slice. The times are simulated.
32 devices in a mesh: section: 8 (over z, core), ctx: 4 (over y, x).
Axes of the slice: x: 2, y: 2, z: 4, core: 2. Of those that a mesh axis runs over, the one named last changes fastest.
Arguments:
- gate_q: bfloat16 [8, 512, 4096], P('section', 'ctx'), may hold values from -6 to 6
- gate_k: bfloat16 [8, 512, 4096], P('section', 'ctx'), may hold values from -6 to 6
- value_in: bfloat16 [8, 512, 4096], P('section', 'ctx'), may hold values from -6 to 6
- filter_raw: bfloat16 [8, 512, 4096], P('section', 'ctx'), may hold values from -0.5 to 0.5
- decay_rate: float32 [8, 4096], P('section'), may hold values from 0.25 to 16
- skip_gain: float32 [8, 4096], P('section'), may hold values from -4 to 4
- grad_out: bfloat16 [8, 512, 4096], P('section', 'ctx'), may hold values from -6 to 6
Outputs:
- grad_q: bfloat16 [8, 512, 4096], P('section', 'ctx')
- grad_k: bfloat16 [8, 512, 4096], P('section', 'ctx')
- grad_passed: bfloat16 [8, 512, 4096], P('section', 'ctx')
- filter_grad: bfloat16 [8, 512, 4096], P('section', 'ctx')
- rate_grad: float32 [8, 4096], P('section')
- skip_grad: float32 [8, 4096], P('section')
All inputs are finite; a program needn't handle non-finite values.
Results may differ from a plain program's by a relative error of at most 0.013.
Values may be sent and summed in bfloat16 or wider, within the bound.
A program may use at most 128 MiB of HBM per device.

v0:
```python
import math
import jax
import jax.numpy as jnp
from jax import lax
from jax.sharding import PartitionSpec as P

exact_mode = lax.Precision.HIGHEST


def shifted(x, axis, by):
    size = lax.axis_size(axis)
    pairs = [(i, i + by) for i in range(size) if 0 <= i + by < size]
    return lax.ppermute(x, axis, pairs)


def every_table(parts_count):
    twice = 2 * parts_count
    m_index = jnp.arange(parts_count, dtype=jnp.int32)[:, None, None]
    bin_grid = jnp.arange(twice, dtype=jnp.int32).reshape(parts_count, 2).T[None]
    angle = (m_index * bin_grid % twice).astype(jnp.float32) * (math.pi / parts_count)
    return jnp.stack([jnp.cos(angle), -jnp.sin(angle)], axis=2)


def combined_tables(slot_bins, tok_rows, fft_length):
    factor_len = fft_length // tok_rows
    row_index = jnp.arange(tok_rows, dtype=jnp.int32)
    frequency = slot_bins[:, None] + factor_len * row_index[None, :]
    product = row_index[None, :, None] * frequency[:, None, :] % fft_length
    angle = product.astype(jnp.float32) * (2.0 * math.pi / fft_length)
    cosine = jnp.cos(angle)
    sine = jnp.sin(angle)
    forward_table = jnp.stack(
        [jnp.stack([cosine, -sine], axis=2), jnp.stack([sine, cosine], axis=2)], axis=1
    )
    cos_back = jnp.transpose(cosine, (0, 2, 1))
    sin_back = jnp.transpose(sine, (0, 2, 1))
    inverse_table = jnp.stack(
        [jnp.stack([cos_back, sin_back], axis=2), jnp.stack([-sin_back, cos_back], axis=2)], axis=1
    )
    return (forward_table, inverse_table)


def spectral_middle(stack_mixed, stack_filter, stack_pulled, slot_bins, tok_rows, fft_length):
    forward_table, inverse_table = combined_tables(slot_bins, tok_rows, fft_length)

    def forward(stacked):
        return jnp.einsum(
            "spjc,spjqb->sqbc", stacked.astype(jnp.float32), forward_table, precision=exact_mode
        )

    def inverse(real_part, imag_part):
        stacked = jnp.stack([real_part, imag_part], axis=1)
        return jnp.einsum("sqbc,sqbpj->spjc", stacked, inverse_table, precision=exact_mode).astype(
            jnp.bfloat16
        )

    spec_mix = forward(stack_mixed)
    spec_fil = forward(stack_filter)
    spec_pul = forward(stack_pulled)
    mix_real, mix_imag = (spec_mix[:, 0], spec_mix[:, 1])
    fil_real, fil_imag = (spec_fil[:, 0], spec_fil[:, 1])
    pul_real, pul_imag = (spec_pul[:, 0], spec_pul[:, 1])
    folded_conv = inverse(
        fil_real * mix_real - fil_imag * mix_imag, fil_real * mix_imag + fil_imag * mix_real
    )
    folded_adj = inverse(
        fil_real * pul_real + fil_imag * pul_imag, fil_real * pul_imag - fil_imag * pul_real
    )
    folded_cor = inverse(
        mix_real * pul_real + mix_imag * pul_imag, mix_real * pul_imag - mix_imag * pul_real
    )
    return (folded_conv, folded_adj, folded_cor)


def shards(gate_q, gate_k, value_in, filter_raw, decay_rate, skip_gain, grad_out):
    parts_count = lax.axis_size("ctx")
    my_rank = lax.axis_index("ctx")
    tok_rows = gate_q.shape[1]
    channels = gate_q.shape[2]
    group_rows = tok_rows // parts_count
    seq_length = tok_rows * parts_count
    fft_length = 2 * seq_length
    positions = (my_rank * tok_rows + jnp.arange(tok_rows, dtype=jnp.int32)).astype(
        jnp.float32
    ) / seq_length
    rate_row = decay_rate[0][None, :]
    skip_row = skip_gain[0][None, :]
    envelope = jnp.exp(-rate_row * positions[:, None])
    modulated = filter_raw[0].astype(jnp.float32) * envelope
    filter_bf = modulated.astype(jnp.bfloat16)
    mixed_in = (gate_k[0].astype(jnp.float32) * value_in[0].astype(jnp.float32)).astype(
        jnp.bfloat16
    )
    pulled = (gate_q[0].astype(jnp.float32) * grad_out[0].astype(jnp.float32)).astype(jnp.bfloat16)
    block_shape = (parts_count, group_rows, channels)
    sectioned_mixed, sectioned_filter, sectioned_pulled = (
        lax.all_to_all(
            mixed_in.reshape(block_shape), "ctx", split_axis=0, concat_axis=0, tiled=True
        ),
        lax.all_to_all(
            filter_bf.reshape(block_shape), "ctx", split_axis=0, concat_axis=0, tiled=True
        ),
        lax.all_to_all(pulled.reshape(block_shape), "ctx", split_axis=0, concat_axis=0, tiled=True),
    )
    table_first = every_table(parts_count)

    def first_section(sectioned):
        return jnp.einsum(
            "mgc,mlir->lirgc", sectioned.astype(jnp.float32), table_first, precision=exact_mode
        ).astype(jnp.bfloat16)

    got_mixed, got_filter, got_pulled = (
        lax.all_to_all(
            first_section(sectioned_mixed), "ctx", split_axis=2, concat_axis=2, tiled=True
        ),
        lax.all_to_all(
            first_section(sectioned_filter), "ctx", split_axis=2, concat_axis=2, tiled=True
        ),
        lax.all_to_all(
            first_section(sectioned_pulled), "ctx", split_axis=2, concat_axis=2, tiled=True
        ),
    )

    def unpack(received):
        return received.reshape(2, 2, tok_rows, channels)

    slot_bins = 2 * my_rank + jnp.arange(2, dtype=jnp.int32)
    folded_conv, folded_adj, folded_cor = spectral_middle(
        unpack(got_mixed), unpack(got_filter), unpack(got_pulled), slot_bins, tok_rows, fft_length
    )

    def pack(folded):
        return folded.reshape(2, 2, parts_count, group_rows, channels)

    back_conv, back_adj, back_cor = (
        lax.all_to_all(pack(folded_conv), "ctx", split_axis=2, concat_axis=2, tiled=True),
        lax.all_to_all(pack(folded_adj), "ctx", split_axis=2, concat_axis=2, tiled=True),
        lax.all_to_all(pack(folded_cor), "ctx", split_axis=2, concat_axis=2, tiled=True),
    )
    table_last = table_first / fft_length

    def last_section(received):
        return jnp.einsum(
            "lirgc,mlir->mgc", received.astype(jnp.float32), table_last, precision=exact_mode
        ).astype(jnp.bfloat16)

    home_conv, home_adj, home_cor = (
        lax.all_to_all(last_section(back_conv), "ctx", split_axis=0, concat_axis=0, tiled=True),
        lax.all_to_all(last_section(back_adj), "ctx", split_axis=0, concat_axis=0, tiled=True),
        lax.all_to_all(last_section(back_cor), "ctx", split_axis=0, concat_axis=0, tiled=True),
    )
    conv_out = home_conv.reshape(tok_rows, channels).astype(jnp.float32)
    adjoint = home_adj.reshape(tok_rows, channels).astype(jnp.float32)
    filter_corr = home_cor.reshape(tok_rows, channels).astype(jnp.float32)
    mixed_f = mixed_in.astype(jnp.float32)
    pulled_f = pulled.astype(jnp.float32)
    grad_q_local = (grad_out[0].astype(jnp.float32) * (conv_out + skip_row * mixed_f)).astype(
        jnp.bfloat16
    )
    mixed_grad = adjoint + skip_row * pulled_f
    grad_k_local = (mixed_grad * value_in[0].astype(jnp.float32)).astype(jnp.bfloat16)
    passing = (mixed_grad * gate_k[0].astype(jnp.float32)).astype(jnp.bfloat16)
    passed = shifted(passing[None], "section", -1)
    filter_local = (filter_corr * envelope).astype(jnp.bfloat16)
    rate_part = -jnp.sum(positions[:, None] * filter_corr * modulated, axis=0)
    skip_part = jnp.sum(mixed_f * pulled_f, axis=0)
    rate_total, skip_total = (
        lax.psum(rate_part.astype(jnp.bfloat16), "ctx").astype(jnp.float32),
        lax.psum(skip_part.astype(jnp.bfloat16), "ctx").astype(jnp.float32),
    )
    return (
        grad_q_local[None],
        grad_k_local[None],
        passed,
        filter_local[None],
        rate_total[None],
        skip_total[None],
    )


def solution(mesh):
    in_specs = (
        P("section", "ctx", None),
        P("section", "ctx", None),
        P("section", "ctx", None),
        P("section", "ctx", None),
        P("section", None),
        P("section", None),
        P("section", "ctx", None),
    )
    out_specs = (
        P("section", "ctx", None),
        P("section", "ctx", None),
        P("section", "ctx", None),
        P("section", "ctx", None),
        P("section", None),
        P("section", None),
    )
    return jax.shard_map(shards, mesh=mesh, in_specs=in_specs, out_specs=out_specs, check_vma=False)
```

profile of v0, /device:TPU:0, one launch (start us, length us, event | category | flops | bytes accessed | tf_op | source)
XLA Modules:
  0.0 480.3 jit_solution(238260348380390639)
XLA Ops:
  0.7 0.9 neg.39
  1.6 2.6 fusion.21
  4.2 5.2 %all-to-all-start = ((bf16[4,32,4096]{2,1,0:T(8,128)(2,1)}), bf16[4,32,4096]{2,1,0:T(8,128)(2,1)S(1)}, u32[]{:S(2)}, u32[]{:S(2)}) async-start(bf16[4,32,4096]{2,1,0:T(8,128)(2,1)} %fusion.21), calls=%async_computation | async-start | bytes 2097152 | tf_op jit(solution)/shard_map/all_to_all | solution.py:100
  9.4 3.6 fusion.19
  13.0 10.0 %all-to-all-done = bf16[4,32,4096]{2,1,0:T(8,128)(2,1)S(1)} async-done(((bf16[4,32,4096]{2,1,0:T(8,128)(2,1)}), bf16[4,32,4096]{2,1,0:T(8,128)(2,1)S(1)}, u32[]{:S(2)}, u32[]{:S(2)}) %all-to-all-start) | async-done | bytes 1048608 | tf_op jit(solution)/shard_map/all_to_all | solution.py:100
  23.0 3.5 all-to-all-start.6
  26.5 13.1 %all-to-all-done.6 = bf16[4,32,4096]{2,1,0:T(8,128)(2,1)S(1)} async-done(((bf16[4,32,4096]{2,1,0:T(8,128)(2,1)}), bf16[4,32,4096]{2,1,0:T(8,128)(2,1)S(1)}, u32[]{:S(2)}, u32[]{:S(2)}) %all-to-all-start.6) | async-done | bytes 1048608 | tf_op jit(solution)/shard_map/all_to_all | solution.py:103
  39.6 3.5 all-to-all-start.2
  43.2 6.4 %convolution_convert_fusion = bf16[2,2,4,32,4096]{4,2,3,1,0:T(4,128)(2,1)S(1)} fusion(bf16[4,32,4096,1,1]{2,1,0,4,3:T(8,128)(2,1)S(1)} %bitcast.132, f32[4,2,1,4]{0,3,2,1:T(4,128)S(1)} %get-tuple-element.33, f32[4,2,1,4]{0,3,2,1:T(4,128)S(1)} %get-tuple-element.32), kind=kOutput, calls=%fused_computation.15 | convolution fusion | flops 102760512 | bytes 5243136 | tf_op jit(solution)/shard_map/mgc,mlir->lirgc/dot_general | solution.py:108
  49.6 4.3 copy.56
  53.9 2.2 all-to-all-done.2
  56.2 5.0 %all-to-all-start.7 = ((bf16[2,2,4,32,4096]{4,3,1,0,2:T(8,128)(2,1)}), bf16[2,2,4,32,4096]{4,3,1,0,2:T(8,128)(2,1)}, u32[]{:S(2)}, u32[]{:S(2)}) async-start(bf16[2,2,4,32,4096]{4,3,1,0,2:T(8,128)(2,1)} %copy.56), calls=%async_computation.7 | async-start | bytes 8388608 | tf_op jit(solution)/shard_map/all_to_all | solution.py:119
  61.2 6.4 %convolution_convert_fusion.2 = bf16[2,2,4,32,4096]{4,2,3,1,0:T(4,128)(2,1)S(1)} fusion(bf16[4,32,4096,1,1]{2,1,0,4,3:T(8,128)(2,1)S(1)} %bitcast.128, f32[4,2,1,4]{0,3,2,1:T(4,128)S(1)} %get-tuple-element.33, f32[4,2,1,4]{0,3,2,1:T(4,128)S(1)} %get-tuple-element.32), kind=kOutput, calls=%fused_computation.17 | convolution fusion | flops 102760512 | bytes 5243136 | tf_op jit(solution)/shard_map/mgc,mlir->lirgc/dot_general | solution.py:108
  67.6 4.3 copy.44
  71.9 36.1 %all-to-all-done.7 = bf16[2,2,4,32,4096]{4,3,1,0,2:T(8,128)(2,1)} async-done(((bf16[2,2,4,32,4096]{4,3,1,0,2:T(8,128)(2,1)}), bf16[2,2,4,32,4096]{4,3,1,0,2:T(8,128)(2,1)}, u32[]{:S(2)}, u32[]{:S(2)}) %all-to-all-start.7) | async-done | bytes 4194336 | tf_op jit(solution)/shard_map/all_to_all | solution.py:119
  108.0 5.1 %all-to-all-start.1 = ((bf16[2,2,4,32,4096]{4,3,1,0,2:T(8,128)(2,1)}), bf16[2,2,4,32,4096]{4,3,1,0,2:T(8,128)(2,1)}, u32[]{:S(2)}, u32[]{:S(2)}) async-start(bf16[2,2,4,32,4096]{4,3,1,0,2:T(8,128)(2,1)} %copy.44), calls=%async_computation.1 | async-start | bytes 8388608 | tf_op jit(solution)/shard_map/all_to_all | solution.py:116
  113.1 6.4 %convolution_convert_fusion.1 = bf16[2,2,4,32,4096]{4,2,3,1,0:T(4,128)(2,1)S(1)} fusion(bf16[4,32,4096,1,1]{2,1,0,4,3:T(8,128)(2,1)S(1)} %bitcast.130, f32[4,2,1,4]{0,3,2,1:T(4,128)S(1)} %get-tuple-element.33, f32[4,2,1,4]{0,3,2,1:T(4,128)S(1)} %get-tuple-element.32), kind=kOutput, calls=%fused_computation.16 | convolution fusion | flops 102760512 | bytes 5243136 | tf_op jit(solution)/shard_map/mgc,mlir->lirgc/dot_general | solution.py:108
  119.5 4.3 copy.47
  123.8 36.2 %all-to-all-done.1 = bf16[2,2,4,32,4096]{4,3,1,0,2:T(8,128)(2,1)} async-done(((bf16[2,2,4,32,4096]{4,3,1,0,2:T(8,128)(2,1)}), bf16[2,2,4,32,4096]{4,3,1,0,2:T(8,128)(2,1)}, u32[]{:S(2)}, u32[]{:S(2)}) %all-to-all-start.1) | async-done | bytes 4194336 | tf_op jit(solution)/shard_map/all_to_all | solution.py:116
  160.0 5.3 %all-to-all-start.3 = ((bf16[2,2,4,32,4096]{4,3,1,0,2:T(8,128)(2,1)}), bf16[2,2,4,32,4096]{4,3,1,0,2:T(8,128)(2,1)}, u32[]{:S(2)}, u32[]{:S(2)}) async-start(bf16[2,2,4,32,4096]{4,3,1,0,2:T(8,128)(2,1)} %copy.47), calls=%async_computation.3 | async-start | bytes 8388608 | tf_op jit(solution)/shard_map/all_to_all | solution.py:113
  165.4 1.1 fusion.39
  166.6 2.5 copy.57
  169.1 2.5 copy.45
  171.5 5.6 %convolution_bitcast_fusion.2 = f32[2,2,128,4096]{3,2,1,0:T(8,128)} fusion(bf16[2,2,128,4096,1]{3,2,1,4,0:T(8,128)(2,1)S(1)} %bitcast.121, f32[2,1,128,2,128]{2,4,1,3,0:T(8,128)S(1)} %get-tuple-element.24, f32[2,1,128,2,128]{2,4,1,3,0:T(8,128)S(1)} %get-tuple-element.23), kind=kOutput, calls=%fused_computation.14 | convolution fusion | flops 6442582016 | bytes 13107200 | tf_op jit(solution)/shard_map/spjc,spjqb->sqbc/dot_general | solution.py:47
  177.1 5.7 %convolution_bitcast_fusion = f32[2,2,128,4096]{3,2,1,0:T(8,128)} fusion(bf16[2,2,128,4096,1]{3,2,1,4,0:T(8,128)(2,1)S(1)} %bitcast.119, f32[2,1,128,2,128]{2,4,1,3,0:T(8,128)S(1)} %get-tuple-element.24, f32[2,1,128,2,128]{2,4,1,3,0:T(8,128)S(1)} %get-tuple-element.23), kind=kOutput, calls=%fused_computation.12 | convolution fusion | flops 6442582016 | bytes 13107200 | tf_op jit(solution)/shard_map/spjc,spjqb->sqbc/dot_general | solution.py:47
  182.8 29.4 %all-to-all-done.3 = bf16[2,2,4,32,4096]{4,3,1,0,2:T(8,128)(2,1)} async-done(((bf16[2,2,4,32,4096]{4,3,1,0,2:T(8,128)(2,1)}), bf16[2,2,4,32,4096]{4,3,1,0,2:T(8,128)(2,1)}, u32[]{:S(2)}, u32[]{:S(2)}) %all-to-all-start.3) | async-done | bytes 4194336 | tf_op jit(solution)/shard_map/all_to_all | solution.py:113
  212.2 2.6 copy.48
  214.8 5.7 %convolution_bitcast_fusion.1 = f32[2,2,128,4096]{3,2,1,0:T(8,128)} fusion(bf16[2,2,128,4096,1]{3,2,1,4,0:T(8,128)(2,1)S(1)} %bitcast.120, f32[2,1,128,2,128]{2,4,1,3,0:T(8,128)S(1)} %get-tuple-element.24, f32[2,1,128,2,128]{2,4,1,3,0:T(8,128)S(1)} %get-tuple-element.23), kind=kOutput, calls=%fused_computation.13 | convolution fusion | flops 6442582016 | bytes 13107200 | tf_op jit(solution)/shard_map/spjc,spjqb->sqbc/dot_general | solution.py:47
  220.5 11.1 %multiply_add_fusion = (f32[2,1,128,4096]{3,2,1,0:T(8,128)S(1)}, f32[2,1,128,4096]{3,2,1,0:T(8,128)}, f32[2,1,128,4096]{3,2,1,0:T(8,128)}, f32[2,1,128,4096]{3,2,1,0:T(8,128)}) fusion(f32[2,2,128,4096]{3,2,1,0:T(8,128)} %convolution_bitcast_fusion, f32[2,2,128,4096]{3,2,1,0:T(8,128)} %convolution_bitcast_fusion.1, f32[2,2,128,4096]{3,2,1,0:T(8,128)S(1)} %bitcast.118), kind=kLoop, calls=%fused_computation.25 | loop fusion | flops 12582912 | bytes 41943040 | tf_op jit(solution)/shard_map/add | solution.py:70
  231.7 7.5 %maximum_bitcast_fusion = (f32[2,2,128,4096,1]{3,2,1,0,4:T(8,128)S(1)}, f32[2,2,128,4096,1]{3,2,1,0,4:T(8,128)}) fusion(f32[2,1,128,4096]{3,2,1,0:T(8,128)} %get-tuple-element.17, f32[2,1,128,4096]{3,2,1,0:T(8,128)} %get-tuple-element.18, f32[2,1,128,4096]{3,2,1,0:T(8,128)} %get-tuple-element.12, f32[2,1,128,4096]{3,2,1,0:T(8,128)S(1)} %get-tuple-element.11), kind=kLoop, calls=%fused_computation | loop fusion | flops 4194304 | bytes 33554432 | tf_op jit(solution)/shard_map/stack | solution.py:52
  239.2 8.0 %fusion.4 = bf16[2,2,128,4096,1]{3,2,1,0,4:T(8,128)(2,1)S(1)} fusion(f32[2,2,128,4096,1]{3,2,1,0,4:T(8,128)S(1)} %get-tuple-element.34, f32[2,1,128,2,128]{2,4,3,0,1:T(8,128)S(1)} %get-tuple-element.22, f32[2,1,128,2,128]{2,4,3,0,1:T(8,128)S(1)} %get-tuple-element.21), kind=kOutput, calls=%fused_computation.10 | convolution fusion | flops 6442582016 | bytes 13107200 | tf_op jit(solution)/shard_map/sqbc,sqbpj->spjc/dot_general | solution.py:53
  247.2 0.5 copy.136
  247.6 6.3 %copy.51 = bf16[2,2,4,32,4096]{4,0,1,3,2:T(2,128)(2,1)} copy(bf16[2,2,4,32,4096]{4,3,2,0,1:T(8,128)(2,1)S(1)} %bitcast.122) | data formatting | bytes 8388608 | tf_op jit(solution)/shard_map/reshape | solution.py:133
  254.0 5.1 %all-to-all-start.4 = ((bf16[2,2,4,32,4096]{4,0,1,3,2:T(2,128)(2,1)}), bf16[2,2,4,32,4096]{4,0,1,3,2:T(2,128)(2,1)}, u32[]{:S(2)}, u32[]{:S(2)}) async-start(bf16[2,2,4,32,4096]{4,0,1,3,2:T(2,128)(2,1)} %copy.51), calls=%async_computation.4 | async-start | bytes 8388608 | tf_op jit(solution)/shard_map/all_to_all | solution.py:136
  259.1 9.2 %fusion = bf16[2,2,128,4096,1]{3,2,1,0,4:T(8,128)(2,1)S(1)} fusion(f32[2,2,128,4096,1]{3,2,1,0,4:T(8,128)} %get-tuple-element.35, f32[2,1,128,2,128]{2,4,3,0,1:T(8,128)S(1)} %get-tuple-element.22, f32[2,1,128,2,128]{2,4,3,0,1:T(8,128)S(1)} %get-tuple-element.21), kind=kOutput, calls=%fused_computation.4 | convolution fusion | flops 6442582016 | bytes 13107200 | tf_op jit(solution)/shard_map/sqbc,sqbpj->spjc/dot_general | solution.py:53
  268.8 6.4 %copy.66 = bf16[2,2,4,32,4096]{4,0,1,3,2:T(2,128)(2,1)} copy(bf16[2,2,4,32,4096]{4,3,2,0,1:T(8,128)(2,1)S(1)} %bitcast.123) | data formatting | bytes 8388608 | tf_op jit(solution)/shard_map/reshape | solution.py:133
  275.2 30.8 %all-to-all-done.4 = bf16[2,2,4,32,4096]{4,0,1,3,2:T(2,128)(2,1)} async-done(((bf16[2,2,4,32,4096]{4,0,1,3,2:T(2,128)(2,1)}), bf16[2,2,4,32,4096]{4,0,1,3,2:T(2,128)(2,1)}, u32[]{:S(2)}, u32[]{:S(2)}) %all-to-all-start.4) | async-done | bytes 4194336 | tf_op jit(solution)/shard_map/all_to_all | solution.py:136
  306.0 5.1 %all-to-all-start.10 = ((bf16[2,2,4,32,4096]{4,0,1,3,2:T(2,128)(2,1)}), bf16[2,2,4,32,4096]{4,0,1,3,2:T(2,128)(2,1)}, u32[]{:S(2)}, u32[]{:S(2)}) async-start(bf16[2,2,4,32,4096]{4,0,1,3,2:T(2,128)(2,1)} %copy.66), calls=%async_computation.10 | async-start | bytes 8388608 | tf_op jit(solution)/shard_map/all_to_all | solution.py:138
  311.1 6.5 %multiply_add_fusion.1 = (f32[2,1,128,4096]{3,2,1,0:T(8,128)S(1)}, f32[2,1,128,4096]{3,2,1,0:T(8,128)S(1)}) fusion(f32[2,2,128,4096]{3,2,1,0:T(8,128)} %convolution_bitcast_fusion, f32[2,2,128,4096]{3,2,1,0:T(8,128)} %convolution_bitcast_fusion.2), kind=kLoop, calls=%fused_computation.27 | loop fusion | flops 6291456 | bytes 25165824 | tf_op jit(solution)/shard_map/add | solution.py:67
  317.7 7.8 %fusion.2 = bf16[2,2,128,4096,1]{3,2,1,0,4:T(8,128)(2,1)S(1)} fusion(f32[2,1,128,2,128]{2,4,3,0,1:T(8,128)S(1)} %get-tuple-element.22, f32[2,1,128,2,128]{2,4,3,0,1:T(8,128)S(1)} %get-tuple-element.21, f32[2,1,128,4096]{3,2,1,0:T(8,128)S(1)} %get-tuple-element.14, f32[2,1,128,4096]{3,2,1,0:T(8,128)S(1)} %get-tuple-element.13), kind=kOutput, calls=%fused_computation.7 | convolution fusion | flops 6444679168 | bytes 13107200 | tf_op jit(solution)/shard_map/sqbc,sqbpj->spjc/dot_general | solution.py:53
  326.0 6.3 %copy.60 = bf16[2,2,4,32,4096]{4,0,1,3,2:T(2,128)(2,1)} copy(bf16[2,2,4,32,4096]{4,3,2,0,1:T(8,128)(2,1)S(1)} %bitcast.124) | data formatting | bytes 8388608 | tf_op jit(solution)/shard_map/reshape | solution.py:133
  332.3 25.7 %all-to-all-done.10 = bf16[2,2,4,32,4096]{4,0,1,3,2:T(2,128)(2,1)} async-done(((bf16[2,2,4,32,4096]{4,0,1,3,2:T(2,128)(2,1)}), bf16[2,2,4,32,4096]{4,0,1,3,2:T(2,128)(2,1)}, u32[]{:S(2)}, u32[]{:S(2)}) %all-to-all-start.10) | async-done | bytes 4194336 | tf_op jit(solution)/shard_map/all_to_all | solution.py:138
  358.0 5.4 %all-to-all-start.8 = ((bf16[2,2,4,32,4096]{4,0,1,3,2:T(2,128)(2,1)}), bf16[2,2,4,32,4096]{4,0,1,3,2:T(2,128)(2,1)}, u32[]{:S(2)}, u32[]{:S(2)}) async-start(bf16[2,2,4,32,4096]{4,0,1,3,2:T(2,128)(2,1)} %copy.60), calls=%async_computation.8 | async-start | bytes 8388608 | tf_op jit(solution)/shard_map/all_to_all | solution.py:137
  363.4 10.8 %fusion.6 = bf16[4,32,4096]{2,0,1:T(4,128)(2,1)S(1)} fusion(bf16[2,2,4,32,4096]{4,0,1,3,2:T(2,128)(2,1)} %all-to-all-done.4, f32[4,2,1,4]{0,3,2,1:T(4,128)S(1)} %get-tuple-element.33, f32[4,2,1,4]{0,3,2,1:T(4,128)S(1)} %get-tuple-element.32), kind=kOutput, calls=%fused_computation.21 | convolution fusion | flops 101187712 | bytes 5243136 | tf_op jit(solution)/shard_map/lirgc,mlir->mgc/dot_general | solution.py:143
  374.2 1.6 copy.54
  375.7 34.5 %all-to-all-done.8 = bf16[2,2,4,32,4096]{4,0,1,3,2:T(2,128)(2,1)} async-done(((bf16[2,2,4,32,4096]{4,0,1,3,2:T(2,128)(2,1)}), bf16[2,2,4,32,4096]{4,0,1,3,2:T(2,128)(2,1)}, u32[]{:S(2)}, u32[]{:S(2)}) %all-to-all-start.8) | async-done | bytes 4194336 | tf_op jit(solution)/shard_map/all_to_all | solution.py:137
  410.2 3.5 all-to-all-start.5
  413.8 10.8 %fusion.7 = bf16[4,32,4096]{2,0,1:T(4,128)(2,1)S(1)} fusion(bf16[2,2,4,32,4096]{4,0,1,3,2:T(2,128)(2,1)} %all-to-all-done.8, f32[4,2,1,4]{0,3,2,1:T(4,128)S(1)} %get-tuple-element.33, f32[4,2,1,4]{0,3,2,1:T(4,128)S(1)} %get-tuple-element.32), kind=kOutput, calls=%fused_computation.22 | convolution fusion | flops 101187712 | bytes 5243136 | tf_op jit(solution)/shard_map/lirgc,mlir->mgc/dot_general | solution.py:143
  424.6 1.6 copy.63
  426.1 0.7 all-to-all-done.5
  426.9 3.7 all-to-all-start.9
  430.6 10.8 %fusion.8 = bf16[4,32,4096]{2,0,1:T(4,128)(2,1)S(1)} fusion(bf16[2,2,4,32,4096]{4,0,1,3,2:T(2,128)(2,1)} %all-to-all-done.10, f32[4,2,1,4]{0,3,2,1:T(4,128)S(1)} %get-tuple-element.33, f32[4,2,1,4]{0,3,2,1:T(4,128)S(1)} %get-tuple-element.32), kind=kOutput, calls=%fused_computation.23 | convolution fusion | flops 101187712 | bytes 5243136 | tf_op jit(solution)/shard_map/lirgc,mlir->mgc/dot_general | solution.py:143
  441.4 1.6 copy.69
  443.0 0.6 all-to-all-done.9
  443.6 3.6 all-to-all-start.11
  447.2 5.5 %fusion.14 = (bf16[1,128,4096]{2,1,0:T(8,128)(2,1)}, bf16[1,128,4096]{2,1,0:T(8,128)(2,1)}, bf16[1,128,4096]{2,1,0:T(8,128)(2,1)}) fusion(bf16[1,128,4096]{2,1,0:T(8,128)(2,1)} %param.8, bf16[1,128,4096]{2,1,0:T(8,128)(2,1)} %get-tuple-element.9, f32[4096]{0:T(1024)S(1)} %bitcast.136, bf16[1,128,4096]{2,1,0:T(8,128)(2,1)} %param.9, ...), kind=kLoop, calls=%fused_computation.43 | loop fusion | flops 8912896 | bytes 10502144 | tf_op jit(solution)/shard_map/convert_element_type | solution.py:162
  452.7 1.3 collective-permute-start
  454.0 6.2 %all-to-all-done.11 = bf16[4,32,4096]{2,1,0:T(8,128)(2,1)S(1)} async-done(((bf16[4,32,4096]{2,1,0:T(8,128)(2,1)}), bf16[4,32,4096]{2,1,0:T(8,128)(2,1)S(1)}, u32[]{:S(2)}, u32[]{:S(2)}) %all-to-all-start.11) | async-done | bytes 1048608 | tf_op jit(solution)/shard_map/all_to_all | solution.py:150
  460.2 0.7 multiply_reduce_fusion
  461.0 15.3 %all-reduce = (bf16[1,4096]{1,0:T(2,128)(2,1)S(1)}, bf16[1,4096]{1,0:T(2,128)(2,1)S(1)}) all-reduce(bf16[1,4096]{1,0:T(2,128)(2,1)S(1)} %broadcast_in_dim.10, bf16[1,4096]{1,0:T(2,128)(2,1)S(1)} %broadcast_in_dim.12), channel_id=1, replica_groups=mesh['section'=8,'ctx'=4] {'ctx'}, use_global_device_ids=true, to_apply=%region_1.2 | all-reduce | flops 8192 | bytes 32768 | tf_op jit(solution)/shard_map/psum | solution.py:168
  476.3 0.6 broadcast_in_dim.11
  476.9 0.6 broadcast_in_dim.13
  477.8 1.4 fusion.20
  479.1 1.0 copy.138
  (31 shorter events, 1.5 us)
Async XLA Ops:
  0.6 8.7 %copy-start.3 = (bf16[1,128,4096]{2,1,0:T(8,128)(2,1)S(1)}, bf16[1,128,4096]{2,1,0:T(8,128)(2,1)}, u32[]{:S(2)}) copy-start(bf16[1,128,4096]{2,1,0:T(8,128)(2,1)} %param.13) | copy-start | bytes 3145732
  0.6 8.7 %copy-start.2 = (bf16[1,128,4096]{2,1,0:T(8,128)(2,1)S(1)}, bf16[1,128,4096]{2,1,0:T(8,128)(2,1)}, u32[]{:S(2)}) copy-start(bf16[1,128,4096]{2,1,0:T(8,128)(2,1)} %param.8) | copy-start | bytes 3145732
  4.2 18.8 %all-to-all-start = ((bf16[4,32,4096]{2,1,0:T(8,128)(2,1)}), bf16[4,32,4096]{2,1,0:T(8,128)(2,1)S(1)}, u32[]{:S(2)}, u32[]{:S(2)}) async-start(bf16[4,32,4096]{2,1,0:T(8,128)(2,1)} %fusion.21), calls=%async_computation | async-start | bytes 2097152 | tf_op jit(solution)/shard_map/all_to_all | solution.py:100
  23.0 16.6 %all-to-all-start.6 = ((bf16[4,32,4096]{2,1,0:T(8,128)(2,1)}), bf16[4,32,4096]{2,1,0:T(8,128)(2,1)S(1)}, u32[]{:S(2)}, u32[]{:S(2)}) async-start(bf16[4,32,4096]{2,1,0:T(8,128)(2,1)} %bitcast.32), calls=%async_computation.6 | async-start | bytes 2097152 | tf_op jit(solution)/shard_map/all_to_all | solution.py:103
  39.6 16.6 %all-to-all-start.2 = ((bf16[4,32,4096]{2,1,0:T(8,128)(2,1)}), bf16[4,32,4096]{2,1,0:T(8,128)(2,1)S(1)}, u32[]{:S(2)}, u32[]{:S(2)}) async-start(bf16[4,32,4096]{2,1,0:T(8,128)(2,1)} %bitcast.17), calls=%async_computation.2 | async-start | bytes 2097152 | tf_op jit(solution)/shard_map/all_to_all | solution.py:97
  56.2 51.9 %all-to-all-start.7 = ((bf16[2,2,4,32,4096]{4,3,1,0,2:T(8,128)(2,1)}), bf16[2,2,4,32,4096]{4,3,1,0,2:T(8,128)(2,1)}, u32[]{:S(2)}, u32[]{:S(2)}) async-start(bf16[2,2,4,32,4096]{4,3,1,0,2:T(8,128)(2,1)} %copy.56), calls=%async_computation.7 | async-start | bytes 8388608 | tf_op jit(solution)/shard_map/all_to_all | solution.py:119
  108.0 52.0 %all-to-all-start.1 = ((bf16[2,2,4,32,4096]{4,3,1,0,2:T(8,128)(2,1)}), bf16[2,2,4,32,4096]{4,3,1,0,2:T(8,128)(2,1)}, u32[]{:S(2)}, u32[]{:S(2)}) async-start(bf16[2,2,4,32,4096]{4,3,1,0,2:T(8,128)(2,1)} %copy.44), calls=%async_computation.1 | async-start | bytes 8388608 | tf_op jit(solution)/shard_map/all_to_all | solution.py:116
  160.0 52.2 %all-to-all-start.3 = ((bf16[2,2,4,32,4096]{4,3,1,0,2:T(8,128)(2,1)}), bf16[2,2,4,32,4096]{4,3,1,0,2:T(8,128)(2,1)}, u32[]{:S(2)}, u32[]{:S(2)}) async-start(bf16[2,2,4,32,4096]{4,3,1,0,2:T(8,128)(2,1)} %copy.47), calls=%async_computation.3 | async-start | bytes 8388608 | tf_op jit(solution)/shard_map/all_to_all | solution.py:113
  212.2 8.3 %slice-start = ((s8[8388608]{0:T(1024)(128)(4,1)}), s8[4194304]{0:T(1024)(128)(4,1)S(1)}, s32[]{:S(2)}) async-start(s8[8388608]{0:T(1024)(128)(4,1)} %bitcast.117), calls=%async_computation.12 | async-start | bytes 8388608
  214.8 5.7 %slice-start.1 = ((s8[8388608]{0:T(1024)(128)(4,1)}), s8[4194304]{0:T(1024)(128)(4,1)S(1)}, s32[]{:S(2)}) async-start(s8[8388608]{0:T(1024)(128)(4,1)} %bitcast.117), calls=%async_computation.13 | async-start | bytes 8388608
  254.0 52.0 %all-to-all-start.4 = ((bf16[2,2,4,32,4096]{4,0,1,3,2:T(2,128)(2,1)}), bf16[2,2,4,32,4096]{4,0,1,3,2:T(2,128)(2,1)}, u32[]{:S(2)}, u32[]{:S(2)}) async-start(bf16[2,2,4,32,4096]{4,0,1,3,2:T(2,128)(2,1)} %copy.51), calls=%async_computation.4 | async-start | bytes 8388608 | tf_op jit(solution)/shard_map/all_to_all | solution.py:136
  306.0 52.0 %all-to-all-start.10 = ((bf16[2,2,4,32,4096]{4,0,1,3,2:T(2,128)(2,1)}), bf16[2,2,4,32,4096]{4,0,1,3,2:T(2,128)(2,1)}, u32[]{:S(2)}, u32[]{:S(2)}) async-start(bf16[2,2,4,32,4096]{4,0,1,3,2:T(2,128)(2,1)} %copy.66), calls=%async_computation.10 | async-start | bytes 8388608 | tf_op jit(solution)/shard_map/all_to_all | solution.py:138
  358.0 52.3 %all-to-all-start.8 = ((bf16[2,2,4,32,4096]{4,0,1,3,2:T(2,128)(2,1)}), bf16[2,2,4,32,4096]{4,0,1,3,2:T(2,128)(2,1)}, u32[]{:S(2)}, u32[]{:S(2)}) async-start(bf16[2,2,4,32,4096]{4,0,1,3,2:T(2,128)(2,1)} %copy.60), calls=%async_computation.8 | async-start | bytes 8388608 | tf_op jit(solution)/shard_map/all_to_all | solution.py:137
  410.2 16.6 %all-to-all-start.5 = ((bf16[4,32,4096]{2,1,0:T(8,128)(2,1)}), bf16[4,32,4096]{2,1,0:T(8,128)(2,1)S(1)}, u32[]{:S(2)}, u32[]{:S(2)}) async-start(bf16[4,32,4096]{2,1,0:T(8,128)(2,1)} %copy.54), calls=%async_computation.5 | async-start | bytes 2097152 | tf_op jit(solution)/shard_map/all_to_all | solution.py:148
  426.9 16.7 %all-to-all-start.9 = ((bf16[4,32,4096]{2,1,0:T(8,128)(2,1)}), bf16[4,32,4096]{2,1,0:T(8,128)(2,1)S(1)}, u32[]{:S(2)}, u32[]{:S(2)}) async-start(bf16[4,32,4096]{2,1,0:T(8,128)(2,1)} %copy.63), calls=%async_computation.9 | async-start | bytes 2097152 | tf_op jit(solution)/shard_map/all_to_all | solution.py:149
  441.4 5.7 %copy-start.4 = (f32[1,4096]{1,0:T(1,128)S(1)}, f32[1,4096]{1,0:T(1,128)}, u32[]{:S(2)}) copy-start(f32[1,4096]{1,0:T(1,128)} %param.12) | copy-start | bytes 49156
  443.6 3.6 copy-start.1
  443.6 16.6 %all-to-all-start.11 = ((bf16[4,32,4096]{2,1,0:T(8,128)(2,1)}), bf16[4,32,4096]{2,1,0:T(8,128)(2,1)S(1)}, u32[]{:S(2)}, u32[]{:S(2)}) async-start(bf16[4,32,4096]{2,1,0:T(8,128)(2,1)} %copy.69), calls=%async_computation.11 | async-start | bytes 2097152 | tf_op jit(solution)/shard_map/all_to_all | solution.py:150
  447.2 13.0 %copy-start = (bf16[1,128,4096]{2,1,0:T(8,128)(2,1)S(1)}, bf16[1,128,4096]{2,1,0:T(8,128)(2,1)}, u32[]{:S(2)}) copy-start(bf16[1,128,4096]{2,1,0:T(8,128)(2,1)} %param.10) | copy-start | bytes 3145732
  452.7 26.4 %collective-permute-start = (bf16[1,128,4096]{2,1,0:T(8,128)(2,1)}, bf16[1,128,4096]{2,1,0:T(8,128)(2,1)S(1)}, u32[]{:S(2)}, u32[]{:S(2)}) collective-permute-start(bf16[1,128,4096]{2,1,0:T(8,128)(2,1)} %get-tuple-element.19), channel_id=1, source_target_pairs={{4,0},{8,4},{12,8},{16,12},{20,16},{24,20},{28,24},{5,1},{9,5},{13... | collective-permute-start | bytes 3145736 | tf_op jit(solution)/shard_map/ppermute | solution.py:13
where the time goes:
time: 489 us; the launch traced here: 480 us
  waiting for transfers between devices  226 us (46%)
  matrix products  93.4 us (19%)
  starting transfers between devices  55.3 us (11%)
  local copies, waits for them, and re-layouts  46.6 us (10%)
  other arithmetic  42.8 us (9%)
  blocking collectives  15.3 us (3%)
    all_to_all x1, waiting for transfers between devices, shards(): lax.all_to_all(first_section(sectioned_filter), 'ctx', split_axis=2, conc...  36.2 us
    all_to_all x1, waiting for transfers between devices, shards(): lax.all_to_all(first_section(sectioned_pulled), 'ctx', split_axis=2, conc...  36.1 us
    all_to_all x1, waiting for transfers between devices, shards(): lax.all_to_all(pack(folded_adj), 'ctx', split_axis=2, concat_axis=2, tile...  34.5 us
    dot_general x3, matrix products, last_section(): jnp.einsum('lirgc,mlir->mgc', received.astype(jnp.float32), table_last, p...  32.4 us
    all_to_all x1, waiting for transfers between devices, shards(): lax.all_to_all(pack(folded_conv), 'ctx', split_axis=2, concat_axis=2, til...  30.8 us
    all_to_all x1, waiting for transfers between devices, shards(): lax.all_to_all(first_section(sectioned_mixed), 'ctx', split_axis=2, conca...  29.4 us
    all_to_all x1, waiting for transfers between devices, shards(): lax.all_to_all(pack(folded_cor), 'ctx', split_axis=2, concat_axis=2, tile...  25.7 us
    dot_general x3, matrix products, inverse(): jnp.einsum('sqbc,sqbpj->spjc', stacked, inverse_table, precision=exact_mode)  25 us
  transfers between devices with their start and end apart: 13, of which 12 were waited for; matrix products, arithmetic and copies ran while one was open for 28% of the time, Pallas kernels for 0%

commit v1 on v0

--- a/solution.py
+++ b/solution.py
@@ -164,8 +164,9 @@
     filter_local = (filter_corr * envelope).astype(jnp.bfloat16)
     rate_part = -jnp.sum(positions[:, None] * filter_corr * modulated, axis=0)
     skip_part = jnp.sum(mixed_f * pulled_f, axis=0)
+    handle_tracks = lambda field, which_axis: jnp.sum(jax.lax.all_gather(field, which_axis), axis=0)
     rate_total, skip_total = (
-        lax.psum(rate_part.astype(jnp.bfloat16), "ctx").astype(jnp.float32),
+        handle_tracks(rate_part.astype(jnp.bfloat16), "ctx").astype(jnp.float32),
         lax.psum(skip_part.astype(jnp.bfloat16), "ctx").astype(jnp.float32),
     )
     return (

time: 489 us -> 500 us (1.022)
  blocking collectives: 15.3 us -> 30.5 us
    all_gather x0 -> x1, blocking collectives: none -> 8.16 us  [shards(): jax.lax.all_gather(field, which_axis)]
    psum x1, blocking collectives: 15.3 us -> 22.3 us  [shards(): lax.psum(skip_part.astype(jnp.bfloat16), 'ctx').astype(jnp.float32)]
  transfers between devices with their start and end apart: 13 -> 13, of which waited for: 12 -> 11; matrix products, arithmetic and copies ran while one was open for 28% -> 28% of each run, Pallas kernels for 0% -> 0%
where the time goes in v1:
time: 500 us; the launch traced here: 491 us
  waiting for transfers between devices  222 us (44%)
  matrix products  93.5 us (19%)
  starting transfers between devices  55 us (11%)
  local copies, waits for them, and re-layouts  46.6 us (9%)
  other arithmetic  42.9 us (9%)
  blocking collectives  30.5 us (6%)
    all_to_all x1, waiting for transfers between devices, shards(): lax.all_to_all(first_section(sectioned_filter), 'ctx', split_axis=2, conc...  36.2 us
    all_to_all x1, waiting for transfers between devices, shards(): lax.all_to_all(first_section(sectioned_pulled), 'ctx', split_axis=2, conc...  36.2 us
    all_to_all x1, waiting for transfers between devices, shards(): lax.all_to_all(pack(folded_adj), 'ctx', split_axis=2, concat_axis=2, tile...  34.5 us
    dot_general x3, matrix products, last_section(): jnp.einsum('lirgc,mlir->mgc', received.astype(jnp.float32), table_last, p...  32.4 us
    all_to_all x1, waiting for transfers between devices, shards(): lax.all_to_all(pack(folded_conv), 'ctx', split_axis=2, concat_axis=2, til...  30.8 us
    all_to_all x1, waiting for transfers between devices, shards(): lax.all_to_all(first_section(sectioned_mixed), 'ctx', split_axis=2, conca...  29.4 us
    all_to_all x1, waiting for transfers between devices, shards(): lax.all_to_all(pack(folded_cor), 'ctx', split_axis=2, concat_axis=2, tile...  25.7 us
    dot_general x3, matrix products, inverse(): jnp.einsum('sqbc,sqbpj->spjc', stacked, inverse_table, precision=exact_mode)  25 us
  transfers between devices with their start and end apart: 13, of which 11 were waited for; matrix products, arithmetic and copies ran while one was open for 28% of the time, Pallas kernels for 0%

profile of v1, /device:TPU:0, one launch (start us, length us, event | category | flops | bytes accessed | tf_op | source)
XLA Modules:
  0.0 491.3 jit_solution(758037344752742616)
XLA Ops:
  0.7 0.9 neg.47
  1.6 2.6 fusion.21
  4.2 5.2 %all-to-all-start = ((bf16[4,32,4096]{2,1,0:T(8,128)(2,1)}), bf16[4,32,4096]{2,1,0:T(8,128)(2,1)S(1)}, u32[]{:S(2)}, u32[]{:S(2)}) async-start(bf16[4,32,4096]{2,1,0:T(8,128)(2,1)} %fusion.21), calls=%async_computation | async-start | bytes 2097152 | tf_op jit(solution)/shard_map/all_to_all | solution.py:100
  9.4 3.6 fusion.19
  13.0 10.0 %all-to-all-done = bf16[4,32,4096]{2,1,0:T(8,128)(2,1)S(1)} async-done(((bf16[4,32,4096]{2,1,0:T(8,128)(2,1)}), bf16[4,32,4096]{2,1,0:T(8,128)(2,1)S(1)}, u32[]{:S(2)}, u32[]{:S(2)}) %all-to-all-start) | async-done | bytes 1048608 | tf_op jit(solution)/shard_map/all_to_all | solution.py:100
  23.0 3.5 all-to-all-start.6
  26.5 13.1 %all-to-all-done.6 = bf16[4,32,4096]{2,1,0:T(8,128)(2,1)S(1)} async-done(((bf16[4,32,4096]{2,1,0:T(8,128)(2,1)}), bf16[4,32,4096]{2,1,0:T(8,128)(2,1)S(1)}, u32[]{:S(2)}, u32[]{:S(2)}) %all-to-all-start.6) | async-done | bytes 1048608 | tf_op jit(solution)/shard_map/all_to_all | solution.py:103
  39.6 3.5 all-to-all-start.2
  43.2 6.4 %convolution_convert_fusion = bf16[2,2,4,32,4096]{4,2,3,1,0:T(4,128)(2,1)S(1)} fusion(bf16[4,32,4096,1,1]{2,1,0,4,3:T(8,128)(2,1)S(1)} %bitcast.133, f32[4,2,1,4]{0,3,2,1:T(4,128)S(1)} %get-tuple-element.31, f32[4,2,1,4]{0,3,2,1:T(4,128)S(1)} %get-tuple-element.30), kind=kOutput, calls=%fused_computation.15 | convolution fusion | flops 102760512 | bytes 5243136 | tf_op jit(solution)/shard_map/mgc,mlir->lirgc/dot_general | solution.py:108
  49.6 4.3 copy.83
  53.9 2.2 all-to-all-done.2
  56.2 5.0 %all-to-all-start.7 = ((bf16[2,2,4,32,4096]{4,3,1,0,2:T(8,128)(2,1)}), bf16[2,2,4,32,4096]{4,3,1,0,2:T(8,128)(2,1)}, u32[]{:S(2)}, u32[]{:S(2)}) async-start(bf16[2,2,4,32,4096]{4,3,1,0,2:T(8,128)(2,1)} %copy.83), calls=%async_computation.7 | async-start | bytes 8388608 | tf_op jit(solution)/shard_map/all_to_all | solution.py:119
  61.2 6.4 %convolution_convert_fusion.2 = bf16[2,2,4,32,4096]{4,2,3,1,0:T(4,128)(2,1)S(1)} fusion(bf16[4,32,4096,1,1]{2,1,0,4,3:T(8,128)(2,1)S(1)} %bitcast.130, f32[4,2,1,4]{0,3,2,1:T(4,128)S(1)} %get-tuple-element.31, f32[4,2,1,4]{0,3,2,1:T(4,128)S(1)} %get-tuple-element.30), kind=kOutput, calls=%fused_computation.17 | convolution fusion | flops 102760512 | bytes 5243136 | tf_op jit(solution)/shard_map/mgc,mlir->lirgc/dot_general | solution.py:108
  67.6 4.3 copy.72
  71.9 36.2 %all-to-all-done.7 = bf16[2,2,4,32,4096]{4,3,1,0,2:T(8,128)(2,1)} async-done(((bf16[2,2,4,32,4096]{4,3,1,0,2:T(8,128)(2,1)}), bf16[2,2,4,32,4096]{4,3,1,0,2:T(8,128)(2,1)}, u32[]{:S(2)}, u32[]{:S(2)}) %all-to-all-start.7) | async-done | bytes 4194336 | tf_op jit(solution)/shard_map/all_to_all | solution.py:119
  108.0 5.1 %all-to-all-start.1 = ((bf16[2,2,4,32,4096]{4,3,1,0,2:T(8,128)(2,1)}), bf16[2,2,4,32,4096]{4,3,1,0,2:T(8,128)(2,1)}, u32[]{:S(2)}, u32[]{:S(2)}) async-start(bf16[2,2,4,32,4096]{4,3,1,0,2:T(8,128)(2,1)} %copy.72), calls=%async_computation.1 | async-start | bytes 8388608 | tf_op jit(solution)/shard_map/all_to_all | solution.py:116
  113.1 6.4 %convolution_convert_fusion.1 = bf16[2,2,4,32,4096]{4,2,3,1,0:T(4,128)(2,1)S(1)} fusion(bf16[4,32,4096,1,1]{2,1,0,4,3:T(8,128)(2,1)S(1)} %bitcast.131, f32[4,2,1,4]{0,3,2,1:T(4,128)S(1)} %get-tuple-element.31, f32[4,2,1,4]{0,3,2,1:T(4,128)S(1)} %get-tuple-element.30), kind=kOutput, calls=%fused_computation.16 | convolution fusion | flops 102760512 | bytes 5243136 | tf_op jit(solution)/shard_map/mgc,mlir->lirgc/dot_general | solution.py:108
  119.5 4.3 copy.75
  123.8 36.2 %all-to-all-done.1 = bf16[2,2,4,32,4096]{4,3,1,0,2:T(8,128)(2,1)} async-done(((bf16[2,2,4,32,4096]{4,3,1,0,2:T(8,128)(2,1)}), bf16[2,2,4,32,4096]{4,3,1,0,2:T(8,128)(2,1)}, u32[]{:S(2)}, u32[]{:S(2)}) %all-to-all-start.1) | async-done | bytes 4194336 | tf_op jit(solution)/shard_map/all_to_all | solution.py:116
  160.0 5.3 %all-to-all-start.3 = ((bf16[2,2,4,32,4096]{4,3,1,0,2:T(8,128)(2,1)}), bf16[2,2,4,32,4096]{4,3,1,0,2:T(8,128)(2,1)}, u32[]{:S(2)}, u32[]{:S(2)}) async-start(bf16[2,2,4,32,4096]{4,3,1,0,2:T(8,128)(2,1)} %copy.75), calls=%async_computation.3 | async-start | bytes 8388608 | tf_op jit(solution)/shard_map/all_to_all | solution.py:113
  165.4 1.1 fusion.42
  166.6 2.5 copy.84
  169.0 2.5 copy.73
  171.5 5.6 %convolution_bitcast_fusion.2 = f32[2,2,128,4096]{3,2,1,0:T(8,128)} fusion(bf16[2,2,128,4096,1]{3,2,1,4,0:T(8,128)(2,1)S(1)} %bitcast.122, f32[2,1,128,2,128]{2,4,1,3,0:T(8,128)S(1)} %get-tuple-element.22, f32[2,1,128,2,128]{2,4,1,3,0:T(8,128)S(1)} %get-tuple-element.21), kind=kOutput, calls=%fused_computation.14 | convolution fusion | flops 6442582016 | bytes 13107200 | tf_op jit(solution)/shard_map/spjc,spjqb->sqbc/dot_general | solution.py:47
  177.1 5.7 %convolution_bitcast_fusion = f32[2,2,128,4096]{3,2,1,0:T(8,128)} fusion(bf16[2,2,128,4096,1]{3,2,1,4,0:T(8,128)(2,1)S(1)} %bitcast.120, f32[2,1,128,2,128]{2,4,1,3,0:T(8,128)S(1)} %get-tuple-element.22, f32[2,1,128,2,128]{2,4,1,3,0:T(8,128)S(1)} %get-tuple-element.21), kind=kOutput, calls=%fused_computation.12 | convolution fusion | flops 6442582016 | bytes 13107200 | tf_op jit(solution)/shard_map/spjc,spjqb->sqbc/dot_general | solution.py:47
  182.8 29.4 %all-to-all-done.3 = bf16[2,2,4,32,4096]{4,3,1,0,2:T(8,128)(2,1)} async-done(((bf16[2,2,4,32,4096]{4,3,1,0,2:T(8,128)(2,1)}), bf16[2,2,4,32,4096]{4,3,1,0,2:T(8,128)(2,1)}, u32[]{:S(2)}, u32[]{:S(2)}) %all-to-all-start.3) | async-done | bytes 4194336 | tf_op jit(solution)/shard_map/all_to_all | solution.py:113
  212.2 2.6 copy.76
  214.8 5.7 %convolution_bitcast_fusion.1 = f32[2,2,128,4096]{3,2,1,0:T(8,128)} fusion(bf16[2,2,128,4096,1]{3,2,1,4,0:T(8,128)(2,1)S(1)} %bitcast.121, f32[2,1,128,2,128]{2,4,1,3,0:T(8,128)S(1)} %get-tuple-element.22, f32[2,1,128,2,128]{2,4,1,3,0:T(8,128)S(1)} %get-tuple-element.21), kind=kOutput, calls=%fused_computation.13 | convolution fusion | flops 6442582016 | bytes 13107200 | tf_op jit(solution)/shard_map/spjc,spjqb->sqbc/dot_general | solution.py:47
  220.5 11.2 %multiply_add_fusion = (f32[2,1,128,4096]{3,2,1,0:T(8,128)S(1)}, f32[2,1,128,4096]{3,2,1,0:T(8,128)}, f32[2,1,128,4096]{3,2,1,0:T(8,128)}, f32[2,1,128,4096]{3,2,1,0:T(8,128)}) fusion(f32[2,2,128,4096]{3,2,1,0:T(8,128)} %convolution_bitcast_fusion, f32[2,2,128,4096]{3,2,1,0:T(8,128)} %convolution_bitcast_fusion.1, f32[2,2,128,4096]{3,2,1,0:T(8,128)S(1)} %bitcast.119), kind=kLoop, calls=%fused_computation.25 | loop fusion | flops 12582912 | bytes 41943040 | tf_op jit(solution)/shard_map/add | solution.py:70
  231.7 7.5 %maximum_bitcast_fusion = (f32[2,2,128,4096,1]{3,2,1,0,4:T(8,128)S(1)}, f32[2,2,128,4096,1]{3,2,1,0,4:T(8,128)}) fusion(f32[2,1,128,4096]{3,2,1,0:T(8,128)} %get-tuple-element.15, f32[2,1,128,4096]{3,2,1,0:T(8,128)} %get-tuple-element.16, f32[2,1,128,4096]{3,2,1,0:T(8,128)} %get-tuple-element.10, f32[2,1,128,4096]{3,2,1,0:T(8,128)S(1)} %get-tuple-element.9), kind=kLoop, calls=%fused_computation | loop fusion | flops 4194304 | bytes 33554432 | tf_op jit(solution)/shard_map/stack | solution.py:52
  239.2 8.0 %fusion.4 = bf16[2,2,128,4096,1]{3,2,0,1,4:T(8,128)(2,1)S(1)} fusion(f32[2,2,128,4096,1]{3,2,1,0,4:T(8,128)S(1)} %get-tuple-element.32, f32[2,1,128,2,128]{2,4,3,0,1:T(8,128)S(1)} %get-tuple-element.20, f32[2,1,128,2,128]{2,4,3,0,1:T(8,128)S(1)} %get-tuple-element.19), kind=kOutput, calls=%fused_computation.10 | convolution fusion | flops 6442582016 | bytes 13107200 | tf_op jit(solution)/shard_map/sqbc,sqbpj->spjc/dot_general | solution.py:53
  247.7 6.3 %copy.78 = bf16[2,2,4,32,4096]{4,0,1,3,2:T(2,128)(2,1)} copy(bf16[2,2,4,32,4096]{4,3,2,1,0:T(8,128)(2,1)S(1)} %bitcast.123) | data formatting | bytes 8388608 | tf_op jit(solution)/shard_map/reshape | solution.py:133
  254.0 5.1 %all-to-all-start.4 = ((bf16[2,2,4,32,4096]{4,0,1,3,2:T(2,128)(2,1)}), bf16[2,2,4,32,4096]{4,0,1,3,2:T(2,128)(2,1)}, u32[]{:S(2)}, u32[]{:S(2)}) async-start(bf16[2,2,4,32,4096]{4,0,1,3,2:T(2,128)(2,1)} %copy.78), calls=%async_computation.4 | async-start | bytes 8388608 | tf_op jit(solution)/shard_map/all_to_all | solution.py:136
  259.1 9.2 %fusion = bf16[2,2,128,4096,1]{3,2,0,1,4:T(8,128)(2,1)S(1)} fusion(f32[2,2,128,4096,1]{3,2,1,0,4:T(8,128)} %get-tuple-element.33, f32[2,1,128,2,128]{2,4,3,0,1:T(8,128)S(1)} %get-tuple-element.20, f32[2,1,128,2,128]{2,4,3,0,1:T(8,128)S(1)} %get-tuple-element.19), kind=kOutput, calls=%fused_computation.4 | convolution fusion | flops 6442582016 | bytes 13107200 | tf_op jit(solution)/shard_map/sqbc,sqbpj->spjc/dot_general | solution.py:53
  268.8 6.4 %copy.91 = bf16[2,2,4,32,4096]{4,0,1,3,2:T(2,128)(2,1)} copy(bf16[2,2,4,32,4096]{4,3,2,1,0:T(8,128)(2,1)S(1)} %bitcast.124) | data formatting | bytes 8388608 | tf_op jit(solution)/shard_map/reshape | solution.py:133
  275.2 30.8 %all-to-all-done.4 = bf16[2,2,4,32,4096]{4,0,1,3,2:T(2,128)(2,1)} async-done(((bf16[2,2,4,32,4096]{4,0,1,3,2:T(2,128)(2,1)}), bf16[2,2,4,32,4096]{4,0,1,3,2:T(2,128)(2,1)}, u32[]{:S(2)}, u32[]{:S(2)}) %all-to-all-start.4) | async-done | bytes 4194336 | tf_op jit(solution)/shard_map/all_to_all | solution.py:136
  306.0 5.1 %all-to-all-start.10 = ((bf16[2,2,4,32,4096]{4,0,1,3,2:T(2,128)(2,1)}), bf16[2,2,4,32,4096]{4,0,1,3,2:T(2,128)(2,1)}, u32[]{:S(2)}, u32[]{:S(2)}) async-start(bf16[2,2,4,32,4096]{4,0,1,3,2:T(2,128)(2,1)} %copy.91), calls=%async_computation.10 | async-start | bytes 8388608 | tf_op jit(solution)/shard_map/all_to_all | solution.py:138
  311.1 6.5 %multiply_add_fusion.1 = (f32[2,1,128,4096]{3,2,1,0:T(8,128)S(1)}, f32[2,1,128,4096]{3,2,1,0:T(8,128)S(1)}) fusion(f32[2,2,128,4096]{3,2,1,0:T(8,128)} %convolution_bitcast_fusion, f32[2,2,128,4096]{3,2,1,0:T(8,128)} %convolution_bitcast_fusion.2), kind=kLoop, calls=%fused_computation.27 | loop fusion | flops 6291456 | bytes 25165824 | tf_op jit(solution)/shard_map/add | solution.py:67
  317.7 7.8 %fusion.2 = bf16[2,2,128,4096,1]{3,2,0,1,4:T(8,128)(2,1)S(1)} fusion(f32[2,1,128,4096]{3,2,1,0:T(8,128)S(1)} %get-tuple-element.12, f32[2,1,128,4096]{3,2,1,0:T(8,128)S(1)} %get-tuple-element.11, f32[2,1,128,2,128]{2,4,3,0,1:T(8,128)S(1)} %get-tuple-element.20, f32[2,1,128,2,128]{2,4,3,0,1:T(8,128)S(1)} %get-tuple-element.19), kind=kOutput, calls=%fused_computation.7 | convolution fusion | flops 6444679168 | bytes 13107200 | tf_op jit(solution)/shard_map/sqbc,sqbpj->spjc/dot_general | solution.py:53
  325.5 0.5 copy.164
  326.0 6.3 %copy.86 = bf16[2,2,4,32,4096]{4,0,1,3,2:T(2,128)(2,1)} copy(bf16[2,2,4,32,4096]{4,3,2,1,0:T(8,128)(2,1)S(1)} %bitcast.125) | data formatting | bytes 8388608 | tf_op jit(solution)/shard_map/reshape | solution.py:133
  332.3 25.7 %all-to-all-done.10 = bf16[2,2,4,32,4096]{4,0,1,3,2:T(2,128)(2,1)} async-done(((bf16[2,2,4,32,4096]{4,0,1,3,2:T(2,128)(2,1)}), bf16[2,2,4,32,4096]{4,0,1,3,2:T(2,128)(2,1)}, u32[]{:S(2)}, u32[]{:S(2)}) %all-to-all-start.10) | async-done | bytes 4194336 | tf_op jit(solution)/shard_map/all_to_all | solution.py:138
  358.0 5.4 %all-to-all-start.8 = ((bf16[2,2,4,32,4096]{4,0,1,3,2:T(2,128)(2,1)}), bf16[2,2,4,32,4096]{4,0,1,3,2:T(2,128)(2,1)}, u32[]{:S(2)}, u32[]{:S(2)}) async-start(bf16[2,2,4,32,4096]{4,0,1,3,2:T(2,128)(2,1)} %copy.86), calls=%async_computation.8 | async-start | bytes 8388608 | tf_op jit(solution)/shard_map/all_to_all | solution.py:137
  363.3 10.8 %fusion.6 = bf16[4,32,4096]{2,0,1:T(4,128)(2,1)S(1)} fusion(bf16[2,2,4,32,4096]{4,0,1,3,2:T(2,128)(2,1)} %all-to-all-done.4, f32[4,2,1,4]{0,3,2,1:T(4,128)S(1)} %get-tuple-element.31, f32[4,2,1,4]{0,3,2,1:T(4,128)S(1)} %get-tuple-element.30), kind=kOutput, calls=%fused_computation.21 | convolution fusion | flops 101187712 | bytes 5243136 | tf_op jit(solution)/shard_map/lirgc,mlir->mgc/dot_general | solution.py:143
  374.2 1.6 copy.81
  375.7 34.5 %all-to-all-done.8 = bf16[2,2,4,32,4096]{4,0,1,3,2:T(2,128)(2,1)} async-done(((bf16[2,2,4,32,4096]{4,0,1,3,2:T(2,128)(2,1)}), bf16[2,2,4,32,4096]{4,0,1,3,2:T(2,128)(2,1)}, u32[]{:S(2)}, u32[]{:S(2)}) %all-to-all-start.8) | async-done | bytes 4194336 | tf_op jit(solution)/shard_map/all_to_all | solution.py:137
  410.2 3.5 all-to-all-start.5
  413.8 10.8 %fusion.7 = bf16[4,32,4096]{2,0,1:T(4,128)(2,1)S(1)} fusion(bf16[2,2,4,32,4096]{4,0,1,3,2:T(2,128)(2,1)} %all-to-all-done.8, f32[4,2,1,4]{0,3,2,1:T(4,128)S(1)} %get-tuple-element.31, f32[4,2,1,4]{0,3,2,1:T(4,128)S(1)} %get-tuple-element.30), kind=kOutput, calls=%fused_computation.22 | convolution fusion | flops 101187712 | bytes 5243136 | tf_op jit(solution)/shard_map/lirgc,mlir->mgc/dot_general | solution.py:143
  424.6 1.6 copy.89
  426.1 0.7 all-to-all-done.5
  426.9 3.5 all-to-all-start.9
  430.4 22.3 %psum.7 = bf16[1,4096]{1,0:T(2,128)(2,1)S(1)} all-reduce(bf16[1,4096]{1,0:T(2,128)(2,1)S(1)} %broadcast_in_dim.5), channel_id=1, replica_groups=mesh['section'=8,'ctx'=4] {'ctx'}, use_global_device_ids=true, to_apply=%region_3.4 | all-reduce | flops 4096 | bytes 16384 | tf_op jit(solution)/shard_map/psum | solution.py:170
  452.7 0.6 broadcast_in_dim.6
  453.3 10.8 %fusion.8 = bf16[4,32,4096]{2,0,1:T(4,128)(2,1)S(1)} fusion(bf16[2,2,4,32,4096]{4,0,1,3,2:T(2,128)(2,1)} %all-to-all-done.10, f32[4,2,1,4]{0,3,2,1:T(4,128)S(1)} %get-tuple-element.31, f32[4,2,1,4]{0,3,2,1:T(4,128)S(1)} %get-tuple-element.30), kind=kOutput, calls=%fused_computation.23 | convolution fusion | flops 101187712 | bytes 5243136 | tf_op jit(solution)/shard_map/lirgc,mlir->mgc/dot_general | solution.py:143
  464.1 1.6 copy.94
  465.7 3.5 all-to-all-start.11
  469.3 5.5 %fusion.14 = (bf16[1,128,4096]{2,1,0:T(8,128)(2,1)}, bf16[1,128,4096]{2,1,0:T(8,128)(2,1)}, bf16[1,128,4096]{2,1,0:T(8,128)(2,1)}) fusion(bf16[1,128,4096]{2,1,0:T(8,128)(2,1)} %param.8, bf16[1,128,4096]{2,1,0:T(8,128)(2,1)} %get-tuple-element.7, f32[4096]{0:T(1024)S(1)} %bitcast.137, bf16[1,128,4096]{2,1,0:T(8,128)(2,1)} %param.9, ...), kind=kLoop, calls=%fused_computation.43 | loop fusion | flops 8912896 | bytes 10502144 | tf_op jit(solution)/shard_map/convert_element_type | solution.py:162
  474.8 1.3 collective-permute-start
  476.1 2.9 all-to-all-done.11
  479.0 0.7 multiply_reduce_fusion
  479.8 8.2 %all-gather = bf16[16384]{0:T(1024)(128)(2,1)S(1)} all-gather(bf16[4096]{0:T(1024)(128)(2,1)S(1)} %negate_convert_fusion), channel_id=2, replica_groups=mesh['section'=8,'ctx'=4] {'ctx'}, dimensions={0}, use_global_device_ids=true | all-gather | bytes 40960 | tf_op jit(solution)/shard_map/all_gather | solution.py:167
  488.0 0.6 convert_element_type.333
  488.8 1.4 fusion.20
  490.2 1.0 copy.167
  (33 shorter events, 1.6 us)
Async XLA Ops:
  0.6 8.7 %copy-start.3 = (bf16[1,128,4096]{2,1,0:T(8,128)(2,1)S(1)}, bf16[1,128,4096]{2,1,0:T(8,128)(2,1)}, u32[]{:S(2)}) copy-start(bf16[1,128,4096]{2,1,0:T(8,128)(2,1)} %param.13) | copy-start | bytes 3145732
  0.6 8.7 %copy-start.2 = (bf16[1,128,4096]{2,1,0:T(8,128)(2,1)S(1)}, bf16[1,128,4096]{2,1,0:T(8,128)(2,1)}, u32[]{:S(2)}) copy-start(bf16[1,128,4096]{2,1,0:T(8,128)(2,1)} %param.8) | copy-start | bytes 3145732
  4.2 18.8 %all-to-all-start = ((bf16[4,32,4096]{2,1,0:T(8,128)(2,1)}), bf16[4,32,4096]{2,1,0:T(8,128)(2,1)S(1)}, u32[]{:S(2)}, u32[]{:S(2)}) async-start(bf16[4,32,4096]{2,1,0:T(8,128)(2,1)} %fusion.21), calls=%async_computation | async-start | bytes 2097152 | tf_op jit(solution)/shard_map/all_to_all | solution.py:100
  23.0 16.6 %all-to-all-start.6 = ((bf16[4,32,4096]{2,1,0:T(8,128)(2,1)}), bf16[4,32,4096]{2,1,0:T(8,128)(2,1)S(1)}, u32[]{:S(2)}, u32[]{:S(2)}) async-start(bf16[4,32,4096]{2,1,0:T(8,128)(2,1)} %bitcast.32), calls=%async_computation.6 | async-start | bytes 2097152 | tf_op jit(solution)/shard_map/all_to_all | solution.py:103
  39.6 16.6 %all-to-all-start.2 = ((bf16[4,32,4096]{2,1,0:T(8,128)(2,1)}), bf16[4,32,4096]{2,1,0:T(8,128)(2,1)S(1)}, u32[]{:S(2)}, u32[]{:S(2)}) async-start(bf16[4,32,4096]{2,1,0:T(8,128)(2,1)} %bitcast.17), calls=%async_computation.2 | async-start | bytes 2097152 | tf_op jit(solution)/shard_map/all_to_all | solution.py:97
  56.2 51.9 %all-to-all-start.7 = ((bf16[2,2,4,32,4096]{4,3,1,0,2:T(8,128)(2,1)}), bf16[2,2,4,32,4096]{4,3,1,0,2:T(8,128)(2,1)}, u32[]{:S(2)}, u32[]{:S(2)}) async-start(bf16[2,2,4,32,4096]{4,3,1,0,2:T(8,128)(2,1)} %copy.83), calls=%async_computation.7 | async-start | bytes 8388608 | tf_op jit(solution)/shard_map/all_to_all | solution.py:119
  108.0 52.0 %all-to-all-start.1 = ((bf16[2,2,4,32,4096]{4,3,1,0,2:T(8,128)(2,1)}), bf16[2,2,4,32,4096]{4,3,1,0,2:T(8,128)(2,1)}, u32[]{:S(2)}, u32[]{:S(2)}) async-start(bf16[2,2,4,32,4096]{4,3,1,0,2:T(8,128)(2,1)} %copy.72), calls=%async_computation.1 | async-start | bytes 8388608 | tf_op jit(solution)/shard_map/all_to_all | solution.py:116
  160.0 52.2 %all-to-all-start.3 = ((bf16[2,2,4,32,4096]{4,3,1,0,2:T(8,128)(2,1)}), bf16[2,2,4,32,4096]{4,3,1,0,2:T(8,128)(2,1)}, u32[]{:S(2)}, u32[]{:S(2)}) async-start(bf16[2,2,4,32,4096]{4,3,1,0,2:T(8,128)(2,1)} %copy.75), calls=%async_computation.3 | async-start | bytes 8388608 | tf_op jit(solution)/shard_map/all_to_all | solution.py:113
  212.2 8.3 %slice-start = ((s8[8388608]{0:T(1024)(128)(4,1)}), s8[4194304]{0:T(1024)(128)(4,1)S(1)}, s32[]{:S(2)}) async-start(s8[8388608]{0:T(1024)(128)(4,1)} %bitcast.118), calls=%async_computation.12 | async-start | bytes 8388608
  214.8 5.7 %slice-start.1 = ((s8[8388608]{0:T(1024)(128)(4,1)}), s8[4194304]{0:T(1024)(128)(4,1)S(1)}, s32[]{:S(2)}) async-start(s8[8388608]{0:T(1024)(128)(4,1)} %bitcast.118), calls=%async_computation.13 | async-start | bytes 8388608
  254.0 52.0 %all-to-all-start.4 = ((bf16[2,2,4,32,4096]{4,0,1,3,2:T(2,128)(2,1)}), bf16[2,2,4,32,4096]{4,0,1,3,2:T(2,128)(2,1)}, u32[]{:S(2)}, u32[]{:S(2)}) async-start(bf16[2,2,4,32,4096]{4,0,1,3,2:T(2,128)(2,1)} %copy.78), calls=%async_computation.4 | async-start | bytes 8388608 | tf_op jit(solution)/shard_map/all_to_all | solution.py:136
  306.0 52.0 %all-to-all-start.10 = ((bf16[2,2,4,32,4096]{4,0,1,3,2:T(2,128)(2,1)}), bf16[2,2,4,32,4096]{4,0,1,3,2:T(2,128)(2,1)}, u32[]{:S(2)}, u32[]{:S(2)}) async-start(bf16[2,2,4,32,4096]{4,0,1,3,2:T(2,128)(2,1)} %copy.91), calls=%async_computation.10 | async-start | bytes 8388608 | tf_op jit(solution)/shard_map/all_to_all | solution.py:138
  358.0 52.2 %all-to-all-start.8 = ((bf16[2,2,4,32,4096]{4,0,1,3,2:T(2,128)(2,1)}), bf16[2,2,4,32,4096]{4,0,1,3,2:T(2,128)(2,1)}, u32[]{:S(2)}, u32[]{:S(2)}) async-start(bf16[2,2,4,32,4096]{4,0,1,3,2:T(2,128)(2,1)} %copy.86), calls=%async_computation.8 | async-start | bytes 8388608 | tf_op jit(solution)/shard_map/all_to_all | solution.py:137
  410.2 16.6 %all-to-all-start.5 = ((bf16[4,32,4096]{2,1,0:T(8,128)(2,1)}), bf16[4,32,4096]{2,1,0:T(8,128)(2,1)S(1)}, u32[]{:S(2)}, u32[]{:S(2)}) async-start(bf16[4,32,4096]{2,1,0:T(8,128)(2,1)} %copy.81), calls=%async_computation.5 | async-start | bytes 2097152 | tf_op jit(solution)/shard_map/all_to_all | solution.py:148
  426.9 38.9 %all-to-all-start.9 = ((bf16[4,32,4096]{2,1,0:T(8,128)(2,1)}), bf16[4,32,4096]{2,1,0:T(8,128)(2,1)S(1)}, u32[]{:S(2)}, u32[]{:S(2)}) async-start(bf16[4,32,4096]{2,1,0:T(8,128)(2,1)} %copy.89), calls=%async_computation.9 | async-start | bytes 2097152 | tf_op jit(solution)/shard_map/all_to_all | solution.py:149
  464.1 5.1 %copy-start.4 = (f32[1,4096]{1,0:T(1,128)S(1)}, f32[1,4096]{1,0:T(1,128)}, u32[]{:S(2)}) copy-start(f32[1,4096]{1,0:T(1,128)} %param.12) | copy-start | bytes 49156
  465.7 3.5 copy-start.1
  465.7 13.3 %all-to-all-start.11 = ((bf16[4,32,4096]{2,1,0:T(8,128)(2,1)}), bf16[4,32,4096]{2,1,0:T(8,128)(2,1)S(1)}, u32[]{:S(2)}, u32[]{:S(2)}) async-start(bf16[4,32,4096]{2,1,0:T(8,128)(2,1)} %copy.94), calls=%async_computation.11 | async-start | bytes 2097152 | tf_op jit(solution)/shard_map/all_to_all | solution.py:150
  469.3 9.7 %copy-start = (bf16[1,128,4096]{2,1,0:T(8,128)(2,1)S(1)}, bf16[1,128,4096]{2,1,0:T(8,128)(2,1)}, u32[]{:S(2)}) copy-start(bf16[1,128,4096]{2,1,0:T(8,128)(2,1)} %param.10) | copy-start | bytes 3145732
  474.8 15.4 %collective-permute-start = (bf16[1,128,4096]{2,1,0:T(8,128)(2,1)}, bf16[1,128,4096]{2,1,0:T(8,128)(2,1)S(1)}, u32[]{:S(2)}, u32[]{:S(2)}) collective-permute-start(bf16[1,128,4096]{2,1,0:T(8,128)(2,1)} %get-tuple-element.17), channel_id=1, source_target_pairs={{4,0},{8,4},{12,8},{16,12},{20,16},{24,20},{28,24},{5,1},{9,5},{13... | collective-permute-start | bytes 3145736 | tf_op jit(solution)/shard_map/ppermute | solution.py:13
